TPU v7x, 256 devices: a whole 4x4x8 slice. The times are simulated.
256 devices in a mesh: rows: 16 (over y_hi, x, core), feat: 16 (over y_lo, z).
Axes of the slice: x: 4, y: 4 (y_hi: 2, y_lo: 2; y = y_hi * 2 + y_lo), z: 8, core: 2. Of those that a mesh axis runs over, the one named last changes fastest.
Arguments:
- features: bfloat16 [3072, 16384], P('rows', 'feat'), may hold values from -0.5 to 0.5
- labels: int32 [3072], P('rows'), may hold values 0 or 1
- posterior: bfloat16 [16384], P('feat'), may hold values from -1 to 1
- prior_prec: float32 [16384], P('feat'), may hold values from 1 to 10
Outputs:
- hessian: float32 [16384, 16384], P('feat', 'rows')
- gradient: float32 [16384], P('feat')
All inputs are finite; a program needn't handle non-finite values. No bound on the sum of `labels` on one device may be relied on, other than what follows from the above.
Results may differ from a plain program's by a relative error of at most 0.003.
Values may be sent and summed in bfloat16 or wider, within the bound.
No kernel may reach another device: no remote copies, remote signals or barrier semaphores. Data moves between devices by JAX's collectives and lax.ppermute only.
A program may use at most 64 MiB of HBM per device.

v0:
```python
import jax
import jax.numpy as jnp
from jax import lax
from jax.sharding import PartitionSpec as P


def sent_to_all(x, axis):
    copies = jnp.broadcast_to(x, (lax.axis_size(axis), *x.shape))
    return lax.all_to_all(copies, axis, split_axis=0, concat_axis=0, tiled=True)


def over_copies(x, axis):
    return sent_to_all(x, axis).sum(axis=0)


def side_by_side(arrays, axis, dim, along):
    columns = [a.reshape(*a.shape[:along], -1) for a in arrays]
    both = jnp.concatenate(columns, axis=along)
    whole, at, finished = (lax.all_gather(both, axis, axis=dim, tiled=True), 0, [])
    for a, column in zip(arrays, columns):
        slab = whole[..., at : at + column.shape[along]]
        finished.append(slab.reshape(*slab.shape[:along], *a.shape[along:]))
        at += column.shape[along]
    return tuple(finished)


def per_device(features, labels, posterior, prior_prec):
    row_count = lax.axis_size("rows")
    feat_count = lax.axis_size("feat")
    row_index = lax.axis_index("rows")
    feat_index = lax.axis_index("feat")
    block_width = features.shape[1]
    col_width = block_width * feat_count // row_count
    partial_value = jnp.dot(features, posterior, preferred_element_type=jnp.float32)
    margins = over_copies(partial_value, "feat")
    chance = jax.nn.sigmoid(margins)
    weight = (chance * (1.0 - chance)).astype(jnp.bfloat16)
    residual = (labels.astype(jnp.float32) - chance).astype(jnp.bfloat16)
    all_rows, all_weight = side_by_side((features, weight), "rows", 0, 1)
    local_grad = jnp.dot(residual, features, preferred_element_type=jnp.float32)
    summed = over_copies(local_grad, "rows")
    gradient = summed - prior_prec * posterior.astype(jnp.float32)
    full_width = lax.all_gather(features, "feat", axis=1, tiled=True)
    column_rows = lax.all_to_all(full_width, "rows", split_axis=1, concat_axis=0, tiled=True)
    weighted = all_weight[:, None] * all_rows
    product = lax.dot_general(
        weighted, column_rows, (((0,), (0,)), ((), ())), preferred_element_type=jnp.float32
    )
    global_rows = feat_index * block_width + jnp.arange(block_width, dtype=jnp.int32)
    global_cols = row_index * col_width + jnp.arange(col_width, dtype=jnp.int32)
    on_diagonal = global_rows[:, None] == global_cols[None, :]
    hessian = product + jnp.where(on_diagonal, prior_prec[:, None], jnp.float32(0.0))
    return (hessian, gradient)


def solution(mesh):
    in_specs = (P("rows", "feat"), P("rows"), P("feat"), P("feat"))
    out_specs = (P("feat", "rows"), P("feat"))
    return jax.shard_map(
        per_device, mesh=mesh, in_specs=in_specs, out_specs=out_specs, check_vma=False
    )
```

profile of v0, /device:TPU:1, one launch (start us, length us, event | category | flops | bytes accessed | tf_op | source)
XLA Modules:
  0.0 242.4 jit_solution(10547593554285213768)
XLA Ops:
  7.2 0.0 all-gather.5.cloned.1.call-start
  7.2 0.7 all-gather.5.cloned.1.call-update
  7.9 0.0 all-gather.3.cloned.1.call-start
  7.9 0.7 reshape.56
  8.6 1.2 fusion.3
  9.9 17.3 %all_to_all.31 = f32[16,1,192]{2,1,0:T(1,128)S(1)} all-to-all(f32[16,1,192]{2,1,0:T(1,128)S(1)} %broadcast_in_dim.21), channel_id=1, replica_groups=mesh['rows'=16,'feat'=16] {'feat'}, dimensions={0} | all-to-all | bytes 24576 | tf_op jit(solution)/shard_map/all_to_all | solution.py:9
  27.2 0.7 subtract_convert_fusion
  27.9 0.2 copy.14
  28.0 1.8 pad_maximum_fusion
  29.8 0.0 all-gather.3.cloned.1.call-update
  29.9 1.2 fusion.4
  31.0 0.7 broadcast_in_dim.24
  31.7 8.8 %all-to-all-start.2 = ((f32[16,1,1024]{2,1,0:T(1,128)}), f32[16,1,1024]{2,1,0:T(1,128)S(1)}, u32[]{:S(2)}, u32[]{:S(2)}) async-start(f32[16,1,1024]{2,1,0:T(1,128)} %broadcast_in_dim.24), calls=%async_computation.2 | async-start | bytes 131072 | tf_op jit(solution)/shard_map/all_to_all | solution.py:9
  40.4 51.4 %all-gather.5.cloned.1.call-done = bf16[192,16384]{1,0:T(8,128)(2,1)} async-done(((bf16[192,1024]{1,0:T(8,128)(2,1)}), bf16[192,16384]{1,0:T(8,128)(2,1)}) %all-gather.5.cloned.1.call-update) | async-done | bytes 6291472 | tf_op jit(solution)/shard_map/all_gather | solution.py:43
  91.9 6.4 %copy.21 = bf16[24,16,8,1024]{3,2,0,1:T(8,128)(2,1)} copy(bf16[24,16,8,1024]{3,2,1,0:T(8,128)(2,1)} %bitcast.16) | data formatting | bytes 12582912 | tf_op jit(solution)/shard_map/all_to_all | solution.py:44
  98.3 0.0 all-to-all-done.2
  98.3 0.0 copy-start
  98.3 0.0 copy-start.1
  98.3 12.1 %all-to-all-start.1 = ((bf16[192,16,1024]{2,0,1:T(8,128)(2,1)}), bf16[192,16,1024]{2,0,1:T(8,128)(2,1)}, u32[]{:S(2)}, u32[]{:S(2)}) async-start(bf16[192,16,1024]{2,0,1:T(8,128)(2,1)} %bitcast.15), calls=%async_computation.1 | async-start | bytes 12582912 | tf_op jit(solution)/shard_map/all_to_all | solution.py:44
  110.4 0.1 reduce_sum.19
  110.5 0.0 copy-done
  110.5 0.0 copy-done.1
  110.5 0.6 multiply_subtract_fusion
  111.1 110.6 %all-gather.3.cloned.1.call-done = bf16[3072,1025]{1,0:T(8,128)(2,1)} async-done(((bf16[192,1025]{1,0:T(8,128)(2,1)}), bf16[3072,1025]{1,0:T(8,128)(2,1)}) %all-gather.3.cloned.1.call-update) | async-done | bytes 6297616 | tf_op jit(solution)/shard_map/all_gather | solution.py:19
  221.7 1.4 slice_reduce_fusion
  223.1 0.0 all-to-all-done.1
  223.1 12.5 %select_add_fusion = f32[1024,1024]{1,0:T(8,128)} fusion(bf16[3072,1024]{1,0:T(8,128)(2,1)} %bitcast.3, bf16[3072,1025]{1,0:T(8,128)(2,1)} %all-gather.3.cloned.1.call-done, bf16[3072]{0:T(1024)(128)(2,1)S(1)} %slice_reduce_fusion, f32[1024]{0:T(1024)S(1)} %copy-done.1, s32[1024]{0:T(1024)S(1)} %get-tuple-element.4, s32[1024]{0:T(1024)S(1)} %get-tuple-element.5), kind=kOutput, calls=%fused_computation.3 | convolution fusion | flops 6448742400 | bytes 16795648 | tf_op jit(solution)/shard_map/dot_general | solution.py:46
  (5 shorter events, 0.1 us)
Async XLA Ops:
  7.2 84.7 %all-gather.5.cloned.1.call-start = ((), (), s32[]{:S(2)}) async-start(), calls=%async_computation.4 | async-start | bytes 6684672 | tf_op jit(solution)/shard_map/all_gather | solution.py:43
  7.9 213.8 %all-gather.3.cloned.1.call-start = ((), (), s32[]{:S(2)}) async-start(), calls=%async_computation.3 | async-start | bytes 7520256 | tf_op jit(solution)/shard_map/all_gather | solution.py:19
  31.7 66.6 %all-to-all-start.2 = ((f32[16,1,1024]{2,1,0:T(1,128)}), f32[16,1,1024]{2,1,0:T(1,128)S(1)}, u32[]{:S(2)}, u32[]{:S(2)}) async-start(f32[16,1,1024]{2,1,0:T(1,128)} %broadcast_in_dim.24), calls=%async_computation.2 | async-start | bytes 131072 | tf_op jit(solution)/shard_map/all_to_all | solution.py:9
  98.3 12.2 %copy-start = (bf16[1024]{0:T(1024)(128)(2,1)S(1)}, bf16[1024]{0:T(1024)(128)(2,1)}, u32[]{:S(2)}) copy-start(bf16[1024]{0:T(1024)(128)(2,1)} %param.6) | copy-start | bytes 6148
  98.3 12.2 %copy-start.1 = (f32[1024]{0:T(1024)S(1)}, f32[1024]{0:T(1024)}, u32[]{:S(2)}) copy-start(f32[1024]{0:T(1024)} %param.7) | copy-start | bytes 12292
  98.3 124.8 %all-to-all-start.1 = ((bf16[192,16,1024]{2,0,1:T(8,128)(2,1)}), bf16[192,16,1024]{2,0,1:T(8,128)(2,1)}, u32[]{:S(2)}, u32[]{:S(2)}) async-start(bf16[192,16,1024]{2,0,1:T(8,128)(2,1)} %bitcast.15), calls=%async_computation.1 | async-start | bytes 12582912 | tf_op jit(solution)/shard_map/all_to_all | solution.py:44
Sparse Core Ops, SparseCore 0:
  9.8 82.0 all-gather.4
  95.2 126.4 all-gather.2
where the time goes:
time: 243 us; the launch traced here: 242 us
  waiting for transfers between devices  163 us (67%)
  starting transfers between devices  21 us (9%)
  blocking collectives  17.3 us (7%)
  matrix products  14.8 us (6%)
  between operations  14.1 us (6%)
  local copies, waits for them, and re-layouts  9.38 us (4%)
  other arithmetic  3.19 us (1%)
    all_gather x1, waiting for transfers between devices, side_by_side(): lax.all_gather(both, axis, axis=dim, tiled=True)  111 us
    all_gather x1, waiting for transfers between devices, per_device(): full_width = lax.all_gather(features, 'feat', axis=1, tiled=True)  51.4 us
    all_to_all x1, blocking collectives, sent_to_all(): return lax.all_to_all(copies, axis, split_axis=0, concat_axis=0, tiled=True)  17.3 us
    dot_general x1, matrix products, per_device(): lax.dot_general(weighted, column_rows, (((0,), (0,)), ((), ())), preferre...  12.5 us
    all_to_all x1, starting transfers between devices, per_device(): lax.all_to_all(full_width, 'rows', split_axis=1, concat_axis=0, tiled=True)  12.1 us
    all_to_all x1, starting transfers between devices, sent_to_all(): return lax.all_to_all(copies, axis, split_axis=0, concat_axis=0, tiled=True)  8.76 us
    all_to_all x1, local copies, waits for them, and re-layouts, per_device(): lax.all_to_all(full_width, 'rows', split_axis=1, concat_axis=0, tiled=True)  6.42 us
  transfers between devices with their start and end apart: 4, of which 2 were waited for; matrix products, arithmetic and copies ran while one was open for 6% of the time, Pallas kernels for 0%

commit v1 on v0

--- a/solution.py
+++ b/solution.py
@@ -40,7 +40,10 @@
     local_grad = jnp.dot(residual, features, preferred_element_type=jnp.float32)
     summed = over_copies(local_grad, "rows")
     gradient = summed - prior_prec * posterior.astype(jnp.float32)
-    full_width = lax.all_gather(features, "feat", axis=1, tiled=True)
+    peers = lax.axis_size("feat")
+    pieces = jnp.stack([features for _ in range(peers)])
+    pieces = lax.all_to_all(pieces, "feat", split_axis=0, concat_axis=0)
+    full_width = jnp.concatenate(pieces, axis=1)
     column_rows = lax.all_to_all(full_width, "rows", split_axis=1, concat_axis=0, tiled=True)
     weighted = all_weight[:, None] * all_rows
     product = lax.dot_general(

time: 243 us -> 305 us (1.26)
  waiting for transfers between devices: 163 us -> 221 us
  blocking collectives: 17.3 us -> 33.1 us
  starting transfers between devices: 21 us -> 10.4 us
    all_to_all x1, waiting for transfers between devices: 0.01 us -> 139 us  [per_device(): pieces = lax.all_to_all(pieces, 'feat', split_axis=0, concat_axis=0)]
    all_gather x1, waiting for transfers between devices: 111 us -> 0.01 us  [side_by_side(): lax.all_gather(both, axis, axis=dim, tiled=True)]
    all_to_all x1, waiting for transfers between devices: 0.01 us -> 82.1 us  [per_device(): lax.all_to_all(full_width, 'rows', split_axis=1, concat_axis=0, tiled=True)]
    all_gather x1 -> x0, waiting for transfers between devices: 51.4 us -> none  [per_device(): full_width = lax.all_gather(features, 'feat', axis=1, tiled=True)]
    all_to_all x1 -> x2, blocking collectives: 17.3 us -> 33.1 us  [sent_to_all(): return lax.all_to_all(copies, axis, split_axis=0, concat_axis=0, tiled=True)]
    all_to_all x1, starting transfers between devices: 12.1 us -> 5.58 us  [per_device(): lax.all_to_all(full_width, 'rows', split_axis=1, concat_axis=0, tiled=True)]
    all_to_all x1 -> x0, local copies, waits for them, and re-layouts: 6.42 us -> none  [per_device(): lax.all_to_all(full_width, 'rows', split_axis=1, concat_axis=0, tiled=True)]
    another operation x0 -> x1, local copies, waits for them, and re-layouts: none -> 4.39 us  [per_device(): pieces = jnp.stack([features for _ in range(peers)])]
  transfers between devices with their start and end apart: 4 -> 3, of which waited for: 2 -> 2; matrix products, arithmetic and copies ran while one was open for 6% -> 1% of each run, Pallas kernels for 0% -> 0%
where the time goes in v1:
time: 305 us; the launch traced here: 302 us
  waiting for transfers between devices  221 us (72%)
  blocking collectives  33.1 us (11%)
  matrix products  14.8 us (5%)
  between operations  14.1 us (5%)
  starting transfers between devices  10.4 us (3%)
  local copies, waits for them, and re-layouts  6.73 us (2%)
    all_to_all x1, waiting for transfers between devices, per_device(): pieces = lax.all_to_all(pieces, 'feat', split_axis=0, concat_axis=0)  139 us
    all_to_all x1, waiting for transfers between devices, per_device(): lax.all_to_all(full_width, 'rows', split_axis=1, concat_axis=0, tiled=True)  82.1 us
    all_to_all x2, blocking collectives, sent_to_all(): return lax.all_to_all(copies, axis, split_axis=0, concat_axis=0, tiled=True)  33.1 us
    dot_general x1, matrix products, per_device(): lax.dot_general(weighted, column_rows, (((0,), (0,)), ((), ())), preferre...  12.4 us
  transfers between devices with their start and end apart: 3, of which 2 were waited for; matrix products, arithmetic and copies ran while one was open for 1% of the time, Pallas kernels for 0%

profile of v1, /device:TPU:1, one launch (start us, length us, event | category | flops | bytes accessed | tf_op | source)
XLA Modules:
  0.0 302.5 jit_solution(15596093347263968525)
XLA Ops:
  7.2 0.7 reshape.64
  7.9 1.2 fusion.3
  9.1 17.3 %all_to_all.33 = f32[16,1,192]{2,1,0:T(1,128)S(1)} all-to-all(f32[16,1,192]{2,1,0:T(1,128)S(1)} %broadcast_in_dim.21), channel_id=1, replica_groups=mesh['rows'=16,'feat'=16] {'feat'}, dimensions={0} | all-to-all | bytes 24576 | tf_op jit(solution)/shard_map/all_to_all | solution.py:9
  26.4 0.7 subtract_convert_fusion
  27.1 1.2 fusion.4
  28.3 15.9 %all_to_all.34 = f32[16,1,1024]{2,1,0:T(1,128)S(1)} all-to-all(f32[16,1,1024]{2,1,0:T(1,128)S(1)} %broadcast_in_dim.24), channel_id=1, replica_groups=mesh['rows'=16,'feat'=16] {'rows'}, dimensions={0} | all-to-all | bytes 131072 | tf_op jit(solution)/shard_map/all_to_all | solution.py:9
  44.2 4.4 %stack.2 = bf16[16,192,1024]{2,1,0:T(8,128)(2,1)} broadcast(bf16[192,1024]{1,0:T(8,128)(2,1)} %param.4), dimensions={1,2} | broadcast | bytes 6684672 | tf_op jit(solution)/shard_map/stack | solution.py:44
  48.6 0.0 copy-start
  48.6 4.8 %all-to-all-start.1 = ((bf16[16,192,1024]{2,1,0:T(8,128)(2,1)}), bf16[16,192,1024]{2,1,0:T(8,128)(2,1)}, u32[]{:S(2)}, u32[]{:S(2)}) async-start(bf16[16,192,1024]{2,1,0:T(8,128)(2,1)} %stack.2), calls=%async_computation.1 | async-start | bytes 12582912 | tf_op jit(solution)/shard_map/all_to_all | solution.py:45
  53.3 0.0 all-gather.2.cloned.1.call-start
  53.4 0.1 copy.9
  53.6 0.0 copy-done
  53.6 0.8 pad_maximum_fusion
  54.4 0.0 all-gather.2.cloned.1.call-update
  54.4 139.0 %all-to-all-done.1 = bf16[16,192,1024]{2,1,0:T(8,128)(2,1)} async-done(((bf16[16,192,1024]{2,1,0:T(8,128)(2,1)}), bf16[16,192,1024]{2,1,0:T(8,128)(2,1)}, u32[]{:S(2)}, u32[]{:S(2)}) %all-to-all-start.1) | async-done | bytes 6291488 | tf_op jit(solution)/shard_map/all_to_all | solution.py:45
  193.3 0.0 copy-start.1
  193.3 0.0 copy-start.2
  193.3 5.6 %all-to-all-start.2 = ((bf16[192,16,1024]{2,0,1:T(8,128)(2,1)}), bf16[192,16,1024]{2,0,1:T(8,128)(2,1)}, u32[]{:S(2)}, u32[]{:S(2)}) async-start(bf16[192,16,1024]{2,0,1:T(8,128)(2,1)} %bitcast.2), calls=%async_computation.2 | async-start | bytes 12582912 | tf_op jit(solution)/shard_map/all_to_all | solution.py:47
  198.9 0.1 reduce_sum.19
  199.0 0.0 copy-done.1
  199.0 0.0 copy-done.2
  199.0 0.6 multiply_subtract_fusion
  199.6 0.0 all-gather.2.cloned.1.call-done
  199.6 1.4 slice_reduce_fusion
  201.0 82.1 %all-to-all-done.2 = bf16[192,16,1024]{2,0,1:T(8,128)(2,1)} async-done(((bf16[192,16,1024]{2,0,1:T(8,128)(2,1)}), bf16[192,16,1024]{2,0,1:T(8,128)(2,1)}, u32[]{:S(2)}, u32[]{:S(2)}) %all-to-all-start.2) | async-done | bytes 6291488 | tf_op jit(solution)/shard_map/all_to_all | solution.py:47
  283.2 12.4 %select_add_fusion = f32[1024,1024]{1,0:T(8,128)} fusion(bf16[3072,1024]{1,0:T(8,128)(2,1)} %bitcast.4, bf16[3072,1025]{1,0:T(8,128)(2,1)} %all-gather.2.cloned.1.call-done, bf16[3072]{0:T(1024)(128)(2,1)S(1)} %slice_reduce_fusion, f32[1024]{0:T(1024)S(1)} %copy-done.2, s32[1024]{0:T(1024)S(1)} %get-tuple-element.4, s32[1024]{0:T(1024)S(1)} %get-tuple-element.5), kind=kOutput, calls=%fused_computation.2 | convolution fusion | flops 6448742400 | bytes 16795648 | tf_op jit(solution)/shard_map/dot_general | solution.py:49
  (6 shorter events, 0.1 us)
Async XLA Ops:
  48.6 5.0 %copy-start = (bf16[192,1024]{1,0:T(8,128)(2,1)S(1)}, bf16[192,1024]{1,0:T(8,128)(2,1)}, u32[]{:S(2)}) copy-start(bf16[192,1024]{1,0:T(8,128)(2,1)} %param.4) | copy-start | bytes 1179652
  48.6 144.8 %all-to-all-start.1 = ((bf16[16,192,1024]{2,1,0:T(8,128)(2,1)}), bf16[16,192,1024]{2,1,0:T(8,128)(2,1)}, u32[]{:S(2)}, u32[]{:S(2)}) async-start(bf16[16,192,1024]{2,1,0:T(8,128)(2,1)} %stack.2), calls=%async_computation.1 | async-start | bytes 12582912 | tf_op jit(solution)/shard_map/all_to_all | solution.py:45
  53.3 146.3 %all-gather.2.cloned.1.call-start = ((), (), s32[]{:S(2)}) async-start(), calls=%async_computation.4 | async-start | bytes 7520256 | tf_op jit(solution)/shard_map/all_gather | solution.py:19
  193.3 5.7 %copy-start.1 = (bf16[1024]{0:T(1024)(128)(2,1)S(1)}, bf16[1024]{0:T(1024)(128)(2,1)}, u32[]{:S(2)}) copy-start(bf16[1024]{0:T(1024)(128)(2,1)} %param.6) | copy-start | bytes 6148
  193.3 5.7 %copy-start.2 = (f32[1024]{0:T(1024)S(1)}, f32[1024]{0:T(1024)}, u32[]{:S(2)}) copy-start(f32[1024]{0:T(1024)} %param.7) | copy-start | bytes 12292
  193.3 89.8 %all-to-all-start.2 = ((bf16[192,16,1024]{2,0,1:T(8,128)(2,1)}), bf16[192,16,1024]{2,0,1:T(8,128)(2,1)}, u32[]{:S(2)}, u32[]{:S(2)}) async-start(bf16[192,16,1024]{2,0,1:T(8,128)(2,1)} %bitcast.2), calls=%async_computation.2 | async-start | bytes 12582912 | tf_op jit(solution)/shard_map/all_to_all | solution.py:47
Sparse Core Ops, SparseCore 0:
  57.5 113.5 all-gather.1

commit v2 on v0

--- a/solution.py
+++ b/solution.py
@@ -41,7 +41,15 @@
     summed = over_copies(local_grad, "rows")
     gradient = summed - prior_prec * posterior.astype(jnp.float32)
     full_width = lax.all_gather(features, "feat", axis=1, tiled=True)
-    column_rows = lax.all_to_all(full_width, "rows", split_axis=1, concat_axis=0, tiled=True)
+    column_rows = jnp.concatenate(
+        lax.all_to_all(
+            jnp.stack(jnp.split(full_width, lax.psum(1, axis_name="rows"), 1), 0),
+            axis_name="rows",
+            split_axis=0,
+            concat_axis=0,
+        ),
+        0,
+    )
     weighted = all_weight[:, None] * all_rows
     product = lax.dot_general(
         weighted, column_rows, (((0,), (0,)), ((), ())), preferred_element_type=jnp.float32

time: 243 us -> 257 us (1.058)
  local copies, waits for them, and re-layouts: 9.38 us -> 31.4 us
  waiting for transfers between devices: 163 us -> 154 us
    unnamed x5 -> x20, local copies, waits for them, and re-layouts: 0.7 us -> 27.3 us
    all_gather x1, waiting for transfers between devices: 111 us -> 102 us  [side_by_side(): lax.all_gather(both, axis, axis=dim, tiled=True)]
    all_to_all x1 -> x0, local copies, waits for them, and re-layouts: 6.42 us -> none  [per_device(): lax.all_to_all(full_width, 'rows', split_axis=1, concat_axis=0, tiled=True)]
  transfers between devices with their start and end apart: 4 -> 4, of which waited for: 2 -> 2; matrix products, arithmetic and copies ran while one was open for 6% -> 14% of each run, Pallas kernels for 0% -> 0%
where the time goes in v2:
time: 257 us; the launch traced here: 256 us
  waiting for transfers between devices  154 us (60%)
  local copies, waits for them, and re-layouts  31.4 us (12%)
  starting transfers between devices  21 us (8%)
  blocking collectives  17.3 us (7%)
  matrix products  14.8 us (6%)
  between operations  14.1 us (5%)
  other arithmetic  3.19 us (1%)
    all_gather x1, waiting for transfers between devices, side_by_side(): lax.all_gather(both, axis, axis=dim, tiled=True)  102 us
    all_gather x1, waiting for transfers between devices, per_device(): full_width = lax.all_gather(features, 'feat', axis=1, tiled=True)  51.4 us
    unnamed x20, local copies, waits for them, and re-layouts  27.3 us
    all_to_all x1, blocking collectives, sent_to_all(): return lax.all_to_all(copies, axis, split_axis=0, concat_axis=0, tiled=True)  17.3 us
    dot_general x1, matrix products, per_device(): lax.dot_general(weighted, column_rows, (((0,), (0,)), ((), ())), preferre...  12.5 us
    all_to_all x1, starting transfers between devices, per_device(): lax.all_to_all(jnp.stack(jnp.split(full_width, lax.psum(1, axis_name='row...  12.2 us
    all_to_all x1, starting transfers between devices, sent_to_all(): return lax.all_to_all(copies, axis, split_axis=0, concat_axis=0, tiled=True)  8.76 us
  transfers between devices with their start and end apart: 4, of which 2 were waited for; matrix products, arithmetic and copies ran while one was open for 14% of the time, Pallas kernels for 0%

profile of v2, /device:TPU:1, one launch (start us, length us, event | category | flops | bytes accessed | tf_op | source)
XLA Modules:
  0.0 255.6 jit_solution(4107302911086472247)
XLA Ops:
  7.2 0.0 all-gather.5.cloned.1.call-start
  7.2 0.7 all-gather.5.cloned.1.call-update
  7.9 0.0 all-gather.3.cloned.1.call-start
  7.9 0.7 reshape.57
  8.6 1.2 fusion.19
  9.9 17.3 %all_to_all.17 = f32[16,1,192]{2,1,0:T(1,128)S(1)} all-to-all(f32[16,1,192]{2,1,0:T(1,128)S(1)} %broadcast_in_dim.21), channel_id=1, replica_groups=mesh['rows'=16,'feat'=16] {'feat'}, dimensions={0} | all-to-all | bytes 24576 | tf_op jit(solution)/shard_map/all_to_all | solution.py:9
  27.2 0.7 subtract_convert_fusion
  27.9 0.2 copy.9
  28.0 1.8 pad_maximum_fusion
  29.8 0.0 all-gather.3.cloned.1.call-update
  29.9 1.2 fusion.20
  31.0 0.7 broadcast_in_dim.24
  31.7 8.8 %all-to-all-start.2 = ((f32[16,1,1024]{2,1,0:T(1,128)}), f32[16,1,1024]{2,1,0:T(1,128)S(1)}, u32[]{:S(2)}, u32[]{:S(2)}) async-start(f32[16,1,1024]{2,1,0:T(1,128)} %broadcast_in_dim.24), calls=%async_computation.2 | async-start | bytes 131072 | tf_op jit(solution)/shard_map/all_to_all | solution.py:9
  40.4 51.4 %all-gather.5.cloned.1.call-done = bf16[192,16384]{1,0:T(8,128)(2,1)} async-done(((bf16[192,1024]{1,0:T(8,128)(2,1)}), bf16[192,16384]{1,0:T(8,128)(2,1)}) %all-gather.5.cloned.1.call-update) | async-done | bytes 6291472 | tf_op jit(solution)/shard_map/all_gather | solution.py:43
  91.9 1.8 fusion.17
  93.7 1.8 fusion.16
  95.4 1.8 fusion.15
  97.2 1.8 fusion.14
  99.0 1.8 fusion.13
  100.8 1.8 fusion.12
  102.5 1.8 fusion.11
  104.3 1.8 fusion.10
  106.1 1.8 fusion.9
  107.8 1.8 fusion.8
  109.6 1.8 fusion.7
  111.4 1.8 fusion.6
  113.2 1.8 fusion.5
  115.0 1.8 fusion.4
  116.7 1.8 fusion.3
  118.5 1.8 fusion.2
  120.3 0.0 copy-start
  120.3 0.0 copy-start.1
  120.3 0.0 all-to-all-done.2
  120.3 12.2 %all-to-all-start.1 = ((bf16[16,192,1024]{2,1,0:T(8,128)(2,1)}), bf16[16,192,1024]{2,1,0:T(8,128)(2,1)}, u32[]{:S(2)}, u32[]{:S(2)}) async-start(bf16[16,192,1024]{2,1,0:T(8,128)(2,1)} %fusion.2), calls=%async_computation.1 | async-start | bytes 12582912 | tf_op jit(solution)/shard_map/all_to_all | solution.py:45
  132.5 0.1 reduce_sum.19
  132.5 0.0 copy-done
  132.6 0.0 copy-done.1
  132.6 0.6 multiply_subtract_fusion
  133.2 101.8 %all-gather.3.cloned.1.call-done = bf16[3072,1025]{1,0:T(8,128)(2,1)} async-done(((bf16[192,1025]{1,0:T(8,128)(2,1)}), bf16[3072,1025]{1,0:T(8,128)(2,1)}) %all-gather.3.cloned.1.call-update) | async-done | bytes 6297616 | tf_op jit(solution)/shard_map/all_gather | solution.py:19
  234.9 1.4 slice_reduce_fusion
  236.3 0.0 all-to-all-done.1
  236.3 12.5 %select_add_fusion = f32[1024,1024]{1,0:T(8,128)} fusion(bf16[3072,1024]{1,0:T(8,128)(2,1)} %bitcast.18, bf16[3072,1025]{1,0:T(8,128)(2,1)} %all-gather.3.cloned.1.call-done, bf16[3072]{0:T(1024)(128)(2,1)S(1)} %slice_reduce_fusion, f32[1024]{0:T(1024)S(1)} %copy-done.1, s32[1024]{0:T(1024)S(1)} %get-tuple-element.4, s32[1024]{0:T(1024)S(1)} %get-tuple-element.5), kind=kOutput, calls=%fused_computation.2 | convolution fusion | flops 6448742400 | bytes 16795648 | tf_op jit(solution)/shard_map/dot_general | solution.py:54
  (5 shorter events, 0.1 us)
Async XLA Ops:
  7.2 84.7 %all-gather.5.cloned.1.call-start = ((), (), s32[]{:S(2)}) async-start(), calls=%async_computation.4 | async-start | bytes 6684672 | tf_op jit(solution)/shard_map/all_gather | solution.py:43
  7.9 227.0 %all-gather.3.cloned.1.call-start = ((), (), s32[]{:S(2)}) async-start(), calls=%async_computation.3 | async-start | bytes 7520256 | tf_op jit(solution)/shard_map/all_gather | solution.py:19
  31.7 88.6 %all-to-all-start.2 = ((f32[16,1,1024]{2,1,0:T(1,128)}), f32[16,1,1024]{2,1,0:T(1,128)S(1)}, u32[]{:S(2)}, u32[]{:S(2)}) async-start(f32[16,1,1024]{2,1,0:T(1,128)} %broadcast_in_dim.24), calls=%async_computation.2 | async-start | bytes 131072 | tf_op jit(solution)/shard_map/all_to_all | solution.py:9
  120.3 12.3 %copy-start = (bf16[1024]{0:T(1024)(128)(2,1)S(1)}, bf16[1024]{0:T(1024)(128)(2,1)}, u32[]{:S(2)}) copy-start(bf16[1024]{0:T(1024)(128)(2,1)} %param.6) | copy-start | bytes 6148
  120.3 12.3 %copy-start.1 = (f32[1024]{0:T(1024)S(1)}, f32[1024]{0:T(1024)}, u32[]{:S(2)}) copy-start(f32[1024]{0:T(1024)} %param.7) | copy-start | bytes 12292
  120.3 116.1 %all-to-all-start.1 = ((bf16[16,192,1024]{2,1,0:T(8,128)(2,1)}), bf16[16,192,1024]{2,1,0:T(8,128)(2,1)}, u32[]{:S(2)}, u32[]{:S(2)}) async-start(bf16[16,192,1024]{2,1,0:T(8,128)(2,1)} %fusion.2), calls=%async_computation.1 | async-start | bytes 12582912 | tf_op jit(solution)/shard_map/all_to_all | solution.py:45
Sparse Core Ops, SparseCore 0:
  9.8 82.0 all-gather.4
  95.2 139.7 all-gather.2
